TPU v7x, 32 devices: a whole 2x2x4 slice. The times are simulated.
32 devices in a mesh: dp: 16 (over z, y, x), mp: 2 (over core).
Axes of the slice: x: 2, y: 2, z: 4, core: 2. Of those that a mesh axis runs over, the one named last changes fastest.
Arguments:
- tokens: bfloat16 [128, 256, 1152], P('dp'), may hold values from -6 to 6
- condition: bfloat16 [128, 1152], P('dp'), may hold values from -6 to 6
- counts: int32 [16], P('dp'), may hold values from 1 to 8, as said below
- w_qkv: bfloat16 [1152, 3, 1152], P(None, None, 'mp'), may hold values from -0.1875 to 0.1875
- b_qv: bfloat16 [2, 1152], P(None, 'mp'), may hold values from -3 to 3
- w_proj: bfloat16 [1152, 1152], P('mp'), may hold values from -0.75 to 0.75
- b_proj: bfloat16 [1152], replicated, may hold values from -3 to 3
- w_up: bfloat16 [1152, 4608], P(None, 'mp'), may hold values from -0.1875 to 0.1875
- b_up: bfloat16 [4608], P('mp'), may hold values from -3 to 3
- w_down: bfloat16 [4608, 1152], P('mp'), may hold values from -0.09375 to 0.09375
- b_down: bfloat16 [1152], replicated, may hold values from -3 to 3
- w_mod: bfloat16 [1152, 6912], P(None, 'mp'), may hold values from -0.1875 to 0.1875
- b_mod: bfloat16 [6912], P('mp'), may hold values from -3 to 3
- cotangent: bfloat16 [128, 256, 1152], P('dp'), may hold values from -6 to 6
Outputs:
- output: bfloat16 [128, 256, 1152], P('dp')
- grad_tokens: float32 [128, 256, 1152], P('dp')
- grad_condition: float32 [128, 1152], P('dp')
- grad_w_qkv: float32 [1152, 3, 1152], P(None, None, 'mp')
- grad_b_qv: float32 [2, 1152], P(None, 'mp')
- grad_w_proj: float32 [1152, 1152], P('mp')
- grad_b_proj: float32 [1152], replicated
- grad_w_up: float32 [1152, 4608], P(None, 'mp')
- grad_b_up: float32 [4608], P('mp')
- grad_w_down: float32 [4608, 1152], P('mp')
- grad_b_down: float32 [1152], replicated
- grad_w_mod: float32 [1152, 6912], P(None, 'mp')
- grad_b_mod: float32 [6912], P('mp')
Inputs may be any that keep to these rules, and one draw needn't show every extreme that they name: counts[g] of group g's 8 slots are live, its first ones; some group has all 8 live in every draw.
All inputs are finite; a program needn't handle non-finite values.
Results may differ from a plain program's by a relative error of at most 0.02.
Values may be sent and summed in bfloat16 or wider, within the bound.
No kernel may reach another device: no remote copies, remote signals or barrier semaphores. Data moves between devices by JAX's collectives and lax.ppermute only.
A program may use at most 256 MiB of HBM per device.

v0:
```python
import jax
import jax.numpy as jnp
from jax import lax
from jax.sharding import PartitionSpec as P

HEAD_DIM = 72
epsilon = 1e-06


def layer_norm(values):
    center = values - jnp.mean(values, axis=-1, keepdims=True)
    return center * lax.rsqrt(jnp.mean(center * center, axis=-1, keepdims=True) + epsilon)


def modulate(values, shift_part, scale_part):
    return layer_norm(values) * (1.0 + scale_part) + shift_part


def gelu_tanh(values):
    return (
        0.5
        * values
        * (1.0 + jnp.tanh(0.7978845608028654 * (values + 0.044715 * values * values * values)))
    )


def inner_rows(left, right):
    return lax.dot_general(
        left, right, (((0,), (0,)), ((), ())), preferred_element_type=jnp.float32
    )


def outer_cols(left, right):
    return lax.dot_general(
        left, right, (((1,), (1,)), ((), ())), preferred_element_type=jnp.float32
    )


def attention_forward(query_rows, key_rows, value_rows):
    factor = HEAD_DIM ** (-0.5)
    scores = (
        jnp.einsum("bqhd,bkhd->bhqk", query_rows, key_rows, preferred_element_type=jnp.float32)
        * factor
    )
    row_max = jnp.max(scores, axis=-1, keepdims=True)
    row_total = jnp.sum(jnp.exp(scores - row_max), axis=-1, keepdims=True)
    logsum = row_max + jnp.log(row_total)
    prob_b = jnp.exp(scores - logsum).astype(jnp.bfloat16)
    mixed_out = jnp.einsum(
        "bhqk,bkhd->bqhd", prob_b, value_rows, preferred_element_type=jnp.float32
    )
    return (mixed_out, logsum)


def attention_backward(query_rows, key_rows, value_rows, logsum, grad_mixed):
    factor = HEAD_DIM ** (-0.5)
    scores = (
        jnp.einsum("bqhd,bkhd->bhqk", query_rows, key_rows, preferred_element_type=jnp.float32)
        * factor
    )
    prob_f = jnp.exp(scores - logsum)
    prob_b = prob_f.astype(jnp.bfloat16)
    grad_prob = jnp.einsum(
        "bqhd,bkhd->bhqk", grad_mixed, value_rows, preferred_element_type=jnp.float32
    )
    row_delta = jnp.sum(prob_f * grad_prob, axis=-1, keepdims=True)
    grad_scores = (prob_f * (grad_prob - row_delta)).astype(jnp.bfloat16)
    grad_query = (
        jnp.einsum("bhqk,bkhd->bqhd", grad_scores, key_rows, preferred_element_type=jnp.float32)
        * factor
    )
    grad_key = (
        jnp.einsum("bhqk,bqhd->bkhd", grad_scores, query_rows, preferred_element_type=jnp.float32)
        * factor
    )
    grad_value = jnp.einsum(
        "bhqk,bqhd->bkhd", prob_b, grad_mixed, preferred_element_type=jnp.float32
    )
    return (
        grad_query.astype(jnp.bfloat16),
        grad_key.astype(jnp.bfloat16),
        grad_value.astype(jnp.bfloat16),
    )


def forward(tokens_f, spans, weights, repeat):
    w_qkv, b_qv, w_proj, b_proj, w_up, b_up, w_down, b_down = weights
    shift_attn, scale_attn, gate_attn, shift_mlp, scale_mlp, gate_mlp = spans
    slot_count, seq_len, model_dim = tokens_f.shape
    row_count = slot_count * seq_len
    head_cols = w_qkv.shape[2]
    head_count = head_cols // HEAD_DIM
    shape_four = (slot_count, seq_len, head_count, HEAD_DIM)
    normed = (
        modulate(tokens_f, shift_attn, scale_attn)
        .astype(jnp.bfloat16)
        .reshape(row_count, model_dim)
    )
    projected = jnp.dot(
        normed, w_qkv.reshape(model_dim, 3 * head_cols), preferred_element_type=jnp.float32
    )
    qkv_bias = jnp.stack([b_qv[0], jnp.zeros_like(b_qv[0]), b_qv[1]]).astype(jnp.float32)
    projected = (projected.reshape(row_count, 3, head_cols) + qkv_bias).astype(jnp.bfloat16)
    query_rows = projected[:, 0].reshape(shape_four)
    key_rows = projected[:, 1].reshape(shape_four)
    value_rows = projected[:, 2].reshape(shape_four)
    mixed_out, logsum = attention_forward(query_rows, key_rows, value_rows)
    mixed_b = mixed_out.astype(jnp.bfloat16).reshape(row_count, head_cols)
    partial_value = jnp.dot(mixed_b, w_proj, preferred_element_type=jnp.float32)
    if repeat:
        summed = lax.psum(partial_value.astype(jnp.bfloat16), "mp").astype(jnp.float32)
    else:
        summed = lax.psum(partial_value.astype(jnp.bfloat16), "mp").astype(jnp.float32)
    attn_out = (summed + b_proj.astype(jnp.float32)).reshape(slot_count, seq_len, model_dim)
    residual = tokens_f + gate_attn * attn_out
    normed_mlp = (
        modulate(residual, shift_mlp, scale_mlp).astype(jnp.bfloat16).reshape(row_count, model_dim)
    )
    hidden = jnp.dot(normed_mlp, w_up, preferred_element_type=jnp.float32) + b_up.astype(
        jnp.float32
    )
    act_bf = gelu_tanh(hidden).astype(jnp.bfloat16)
    partial_mlp = jnp.dot(act_bf, w_down, preferred_element_type=jnp.float32)
    if repeat:
        summed_mlp = lax.psum(partial_mlp.astype(jnp.bfloat16), "mp").astype(jnp.float32)
    else:
        summed_mlp = lax.psum(partial_mlp.astype(jnp.bfloat16), "mp").astype(jnp.float32)
    mlp_out = (summed_mlp + b_down.astype(jnp.float32)).reshape(slot_count, seq_len, model_dim)
    output = residual + gate_mlp * mlp_out
    return {
        "normed": normed,
        "query_rows": query_rows,
        "key_rows": key_rows,
        "value_rows": value_rows,
        "logsum": logsum,
        "mixed_b": mixed_b,
        "attn_out": attn_out,
        "residual": residual,
        "normed_mlp": normed_mlp,
        "hidden": hidden,
        "act_bf": act_bf,
        "mlp_out": mlp_out,
        "output": output,
    }


def image_pass(tokens_f, grad_out, spans, weights):
    w_qkv, b_qv, w_proj, b_proj, w_up, b_up, w_down, b_down = weights
    shift_attn, scale_attn, gate_attn, shift_mlp, scale_mlp, gate_mlp = spans
    slot_count, seq_len, model_dim = tokens_f.shape
    row_count = slot_count * seq_len
    head_cols = w_qkv.shape[2]
    head_count = head_cols // HEAD_DIM
    kept_fwd = forward(tokens_f, spans, weights, False)
    out_one = kept_fwd["output"]
    stored = forward(tokens_f, spans, weights, True)
    grad_gate_mlp = jnp.sum(grad_out * stored["mlp_out"], axis=1)
    grad_mlp = (gate_mlp * grad_out).astype(jnp.bfloat16).reshape(row_count, model_dim)
    grad_b_down = jnp.sum(grad_mlp.astype(jnp.float32), axis=0)
    grad_w_down = inner_rows(stored["act_bf"], grad_mlp)
    grad_act = outer_cols(grad_mlp, w_down)
    gelu_value, gelu_back = jax.vjp(gelu_tanh, stored["hidden"])
    grad_hidden = gelu_back(grad_act)[0].astype(jnp.bfloat16)
    grad_b_up = jnp.sum(grad_hidden.astype(jnp.float32), axis=0)
    grad_w_up = inner_rows(stored["normed_mlp"], grad_hidden)
    part_normed_mlp = outer_cols(grad_hidden, w_up)
    grad_normed_mlp = (
        lax.psum(part_normed_mlp.astype(jnp.bfloat16), "mp")
        .astype(jnp.float32)
        .reshape(slot_count, seq_len, model_dim)
    )
    norm_value, norm_back = jax.vjp(modulate, stored["residual"], shift_mlp, scale_mlp)
    grad_resid_norm, grad_shift_mlp, grad_scale_mlp = norm_back(grad_normed_mlp)
    grad_residual = grad_out + grad_resid_norm
    grad_gate_attn = jnp.sum(grad_residual * stored["attn_out"], axis=1)
    grad_attn = (gate_attn * grad_residual).astype(jnp.bfloat16).reshape(row_count, model_dim)
    grad_b_proj = jnp.sum(grad_attn.astype(jnp.float32), axis=0)
    grad_w_proj = inner_rows(stored["mixed_b"], grad_attn)
    grad_mixed = (
        outer_cols(grad_attn, w_proj)
        .astype(jnp.bfloat16)
        .reshape(slot_count, seq_len, head_count, HEAD_DIM)
    )
    grad_query, grad_key, grad_value = attention_backward(
        stored["query_rows"], stored["key_rows"], stored["value_rows"], stored["logsum"], grad_mixed
    )
    grad_qkv = jnp.stack(
        [
            grad_query.reshape(row_count, head_cols),
            grad_key.reshape(row_count, head_cols),
            grad_value.reshape(row_count, head_cols),
        ],
        axis=1,
    )
    grad_b_qv = jnp.stack(
        [
            jnp.sum(grad_qkv[:, 0].astype(jnp.float32), axis=0),
            jnp.sum(grad_qkv[:, 2].astype(jnp.float32), axis=0),
        ]
    )
    grad_w_qkv = inner_rows(stored["normed"], grad_qkv)
    part_normed = outer_cols(
        grad_qkv.reshape(row_count, 3 * head_cols), w_qkv.reshape(model_dim, 3 * head_cols)
    )
    grad_normed = (
        lax.psum(part_normed.astype(jnp.bfloat16), "mp")
        .astype(jnp.float32)
        .reshape(slot_count, seq_len, model_dim)
    )
    first_value, first_back = jax.vjp(modulate, tokens_f, shift_attn, scale_attn)
    grad_tok_norm, grad_shift_attn, grad_scale_attn = first_back(grad_normed)
    grad_tok_one = grad_residual + grad_tok_norm
    grad_mod_one = jnp.concatenate(
        [
            grad_shift_attn[:, 0],
            grad_scale_attn[:, 0],
            grad_gate_attn,
            grad_shift_mlp[:, 0],
            grad_scale_mlp[:, 0],
            grad_gate_mlp,
        ],
        axis=1,
    )
    grad_terms = (
        grad_w_qkv,
        grad_b_qv,
        grad_w_proj,
        grad_b_proj,
        grad_w_up,
        grad_b_up,
        grad_w_down,
        grad_b_down,
    )
    return (out_one, grad_tok_one, grad_mod_one, grad_terms)


def run_layer(tokens, condition, cotangent, live_count, turns, weights, w_mod, b_mod):
    slot_count, seq_len, model_dim = tokens.shape
    cond_f = condition.astype(jnp.float32)
    scaled = jax.nn.silu(cond_f).astype(jnp.bfloat16)
    own_mod = jnp.dot(scaled, w_mod, preferred_element_type=jnp.float32) + b_mod.astype(jnp.float32)
    modulation = lax.all_gather(own_mod, "mp", axis=1, tiled=True)
    tokens_f = tokens.astype(jnp.float32)
    cot_f = cotangent.astype(jnp.float32)

    def image_step(slot_idx, carry):
        out_buf, grad_buf, mod_buf, grad_sums = carry
        live_flag = (slot_idx < live_count).astype(jnp.float32)
        tok_one = lax.dynamic_slice_in_dim(tokens_f, slot_idx, 1, 0)
        cot_one = lax.dynamic_slice_in_dim(cot_f, slot_idx, 1, 0) * live_flag
        mod_row = lax.dynamic_slice_in_dim(modulation, slot_idx, 1, 0)
        spans = [
            mod_row[:, None, part_idx * model_dim : (part_idx + 1) * model_dim]
            for part_idx in range(6)
        ]
        out_one, grad_tok_one, grad_mod_one, grad_terms = image_pass(
            tok_one, cot_one, spans, weights
        )
        out_one = (out_one * live_flag).astype(jnp.bfloat16)
        out_buf = lax.dynamic_update_slice_in_dim(out_buf, out_one, slot_idx, 0)
        grad_buf = lax.dynamic_update_slice_in_dim(grad_buf, grad_tok_one, slot_idx, 0)
        mod_buf = lax.dynamic_update_slice_in_dim(mod_buf, grad_mod_one, slot_idx, 0)
        grad_sums = tuple((total_a + term_b for total_a, term_b in zip(grad_sums, grad_terms)))
        return (out_buf, grad_buf, mod_buf, grad_sums)

    start_sums = tuple((jnp.zeros(weight_in.shape, jnp.float32) for weight_in in weights))
    start_state = (
        jnp.zeros(tokens.shape, jnp.bfloat16),
        jnp.zeros(tokens.shape, jnp.float32),
        jnp.zeros((slot_count, 6 * model_dim), jnp.float32),
        start_sums,
    )
    out_buf, grad_buf, mod_buf, grad_sums = lax.fori_loop(0, turns, image_step, start_state)
    grad_modulation = mod_buf.astype(jnp.bfloat16)
    own_cols = w_mod.shape[1]
    grad_own = lax.dynamic_slice_in_dim(
        grad_modulation, lax.axis_index("mp") * own_cols, own_cols, 1
    )
    part_scaled = outer_cols(grad_own, w_mod)
    grad_scaled = lax.psum(part_scaled.astype(jnp.bfloat16), "mp").astype(jnp.float32)
    silu_value, silu_back = jax.vjp(jax.nn.silu, cond_f)
    grad_condition = silu_back(grad_scaled)[0]
    return (out_buf, grad_buf, grad_condition, grad_sums, scaled, grad_own)


def on_device(
    tokens,
    condition,
    counts,
    w_qkv,
    b_qv,
    w_proj,
    b_proj,
    w_up,
    b_up,
    w_down,
    b_down,
    w_mod,
    b_mod,
    cotangent,
):
    slot_count, seq_len, model_dim = tokens.shape
    weights = (w_qkv, b_qv, w_proj, b_proj, w_up, b_up, w_down, b_down)
    own_count = counts[0]
    output, grad_tokens, grad_condition, grad_sums, scaled, grad_own = run_layer(
        tokens, condition, cotangent, own_count, slot_count, weights, w_mod, b_mod
    )
    (
        grad_w_qkv,
        grad_b_qv,
        grad_w_proj,
        grad_b_proj,
        grad_w_up,
        grad_b_up,
        grad_w_down,
        grad_b_down,
    ) = grad_sums
    grad_w_mod = inner_rows(scaled, grad_own)
    grad_b_mod = jnp.sum(grad_own.astype(jnp.float32), axis=0)
    (
        grad_w_qkv,
        grad_b_qv,
        grad_w_proj,
        grad_b_proj,
        grad_w_up,
        grad_b_up,
        grad_w_down,
        grad_b_down,
        grad_w_mod,
        grad_b_mod,
    ) = (
        lax.psum(grad_w_qkv.astype(jnp.bfloat16), "dp").astype(jnp.float32),
        lax.psum(grad_b_qv.astype(jnp.bfloat16), "dp").astype(jnp.float32),
        lax.psum(grad_w_proj.astype(jnp.bfloat16), "dp").astype(jnp.float32),
        lax.psum(grad_b_proj.astype(jnp.bfloat16), "dp").astype(jnp.float32),
        lax.psum(grad_w_up.astype(jnp.bfloat16), "dp").astype(jnp.float32),
        lax.psum(grad_b_up.astype(jnp.bfloat16), "dp").astype(jnp.float32),
        lax.psum(grad_w_down.astype(jnp.bfloat16), "dp").astype(jnp.float32),
        lax.psum(grad_b_down.astype(jnp.bfloat16), "dp").astype(jnp.float32),
        lax.psum(grad_w_mod.astype(jnp.bfloat16), "dp").astype(jnp.float32),
        lax.psum(grad_b_mod.astype(jnp.bfloat16), "dp").astype(jnp.float32),
    )
    return (
        output,
        grad_tokens,
        grad_condition,
        grad_w_qkv,
        grad_b_qv,
        grad_w_proj,
        grad_b_proj,
        grad_w_up,
        grad_b_up,
        grad_w_down,
        grad_b_down,
        grad_w_mod,
        grad_b_mod,
    )


def solution(mesh):
    placed = (
        P("dp", None, None),
        P("dp", None),
        P("dp"),
        P(None, None, "mp"),
        P(None, "mp"),
        P("mp", None),
        P(),
        P(None, "mp"),
        P("mp"),
        P("mp", None),
        P(),
        P(None, "mp"),
        P("mp"),
        P("dp", None, None),
    )
    return jax.shard_map(
        on_device,
        mesh=mesh,
        in_specs=placed,
        out_specs=(
            P("dp", None, None),
            P("dp", None, None),
            P("dp", None),
            P(None, None, "mp"),
            P(None, "mp"),
            P("mp", None),
            P(),
            P(None, "mp"),
            P("mp"),
            P("mp", None),
            P(),
            P(None, "mp"),
            P("mp"),
        ),
        check_vma=False,
    )
```

profile of v0, /device:TPU:0, one launch (start us, length us, event | category | flops | bytes accessed | tf_op | source)
XLA Modules:
  0.0 1665.7 jit_solution(14494195875991652209)
XLA Ops:
  8.1 7.3 convert_element_type.373
  23.1 950.2 %while.34 = (s32[]{:T(128)}, bf16[8,256,1152]{2,1,0:T(8,128)(2,1)}, f32[8,256,1152]{2,1,0:T(8,128)}, bf16[8,6912]{1,0:T(8,128)(2,1)}, f32[1152,3,576]{0,2,1:T(8,...) while((s32[]{:T(128)}, bf16[8,256,1152]{2,1,0:T(8,128)(2,1)}, ...), condition=%wide.region_27.0_spmd.clone, body=%wide.region_0.27_spmd.clone.sunk | while | flops 12777392128 | bytes 295346112 | solution.py:273
  38.1 18.6 %all-reduce.12.cloned.1.call-done = bf16[256,1152]{1,0:T(8,128)(2,1)} async-done(((bf16[256,1152]{1,0:T(8,128)(2,1)}), bf16[256,1152]{1,0:T(8,128)(2,1)}) %all-reduce.12.cloned.1.call-update) | async-done | bytes 589840 | tf_op jit(solution)/shard_map/while/body/eval_jaxpr/psum | solution.py:113
  63.3 6.4 convert_reduce_fusion.14
  73.5 7.3 convolution_add_fusion.11
  80.8 5.4 convolution_add_fusion.12
  88.8 4.7 all-reduce.14.cloned.1.call-done
  105.1 4.7 fusion.180
  111.9 6.0 select_add_fusion.8
  118.0 13.0 all-reduce.16.cloned.1.call-done
  157.3 17.2 %all-reduce.12.cloned.1.call-done = bf16[256,1152]{1,0:T(8,128)(2,1)} async-done(((bf16[256,1152]{1,0:T(8,128)(2,1)}), bf16[256,1152]{1,0:T(8,128)(2,1)}) %all-reduce.12.cloned.1.call-update) | async-done | bytes 589840 | tf_op jit(solution)/shard_map/while/body/eval_jaxpr/psum | solution.py:113
  181.0 6.4 convert_reduce_fusion.14
  191.2 10.4 convolution_add_fusion.11
  201.6 7.9 convolution_add_fusion.12
  223.8 4.7 fusion.180
  232.4 8.7 select_add_fusion.8
  241.1 8.5 all-reduce.16.cloned.1.call-done
  276.0 17.2 %all-reduce.12.cloned.1.call-done = bf16[256,1152]{1,0:T(8,128)(2,1)} async-done(((bf16[256,1152]{1,0:T(8,128)(2,1)}), bf16[256,1152]{1,0:T(8,128)(2,1)}) %all-reduce.12.cloned.1.call-update) | async-done | bytes 589840 | tf_op jit(solution)/shard_map/while/body/eval_jaxpr/psum | solution.py:113
  299.7 6.4 convert_reduce_fusion.14
  309.9 10.4 convolution_add_fusion.11
  320.3 7.9 convolution_add_fusion.12
  342.4 4.7 fusion.180
  351.1 8.7 select_add_fusion.8
  359.8 8.5 all-reduce.16.cloned.1.call-done
  394.6 17.2 %all-reduce.12.cloned.1.call-done = bf16[256,1152]{1,0:T(8,128)(2,1)} async-done(((bf16[256,1152]{1,0:T(8,128)(2,1)}), bf16[256,1152]{1,0:T(8,128)(2,1)}) %all-reduce.12.cloned.1.call-update) | async-done | bytes 589840 | tf_op jit(solution)/shard_map/while/body/eval_jaxpr/psum | solution.py:113
  418.4 6.4 convert_reduce_fusion.14
  428.6 10.4 convolution_add_fusion.11
  439.0 7.9 convolution_add_fusion.12
  461.1 4.7 fusion.180
  469.8 8.7 select_add_fusion.8
  478.5 8.5 all-reduce.16.cloned.1.call-done
  513.3 17.2 %all-reduce.12.cloned.1.call-done = bf16[256,1152]{1,0:T(8,128)(2,1)} async-done(((bf16[256,1152]{1,0:T(8,128)(2,1)}), bf16[256,1152]{1,0:T(8,128)(2,1)}) %all-reduce.12.cloned.1.call-update) | async-done | bytes 589840 | tf_op jit(solution)/shard_map/while/body/eval_jaxpr/psum | solution.py:113
  537.1 6.4 convert_reduce_fusion.14
  547.3 10.4 convolution_add_fusion.11
  557.7 7.9 convolution_add_fusion.12
  588.5 8.7 select_add_fusion.8
  597.2 8.5 all-reduce.16.cloned.1.call-done
  632.0 17.2 %all-reduce.12.cloned.1.call-done = bf16[256,1152]{1,0:T(8,128)(2,1)} async-done(((bf16[256,1152]{1,0:T(8,128)(2,1)}), bf16[256,1152]{1,0:T(8,128)(2,1)}) %all-reduce.12.cloned.1.call-update) | async-done | bytes 589840 | tf_op jit(solution)/shard_map/while/body/eval_jaxpr/psum | solution.py:113
  655.8 6.4 convert_reduce_fusion.14
  665.9 10.4 convolution_add_fusion.11
  676.3 7.9 convolution_add_fusion.12
  707.2 8.7 select_add_fusion.8
  715.9 8.5 all-reduce.16.cloned.1.call-done
  750.7 17.2 %all-reduce.12.cloned.1.call-done = bf16[256,1152]{1,0:T(8,128)(2,1)} async-done(((bf16[256,1152]{1,0:T(8,128)(2,1)}), bf16[256,1152]{1,0:T(8,128)(2,1)}) %all-reduce.12.cloned.1.call-update) | async-done | bytes 589840 | tf_op jit(solution)/shard_map/while/body/eval_jaxpr/psum | solution.py:113
  774.4 6.4 convert_reduce_fusion.14
  784.6 10.4 convolution_add_fusion.11
  795.0 7.9 convolution_add_fusion.12
  825.8 8.7 select_add_fusion.8
  834.5 8.5 all-reduce.16.cloned.1.call-done
  869.4 17.2 %all-reduce.12.cloned.1.call-done = bf16[256,1152]{1,0:T(8,128)(2,1)} async-done(((bf16[256,1152]{1,0:T(8,128)(2,1)}), bf16[256,1152]{1,0:T(8,128)(2,1)}) %all-reduce.12.cloned.1.call-update) | async-done | bytes 589840 | tf_op jit(solution)/shard_map/while/body/eval_jaxpr/psum | solution.py:113
  893.1 6.4 convert_reduce_fusion.14
  903.3 10.4 convolution_add_fusion.11
  913.7 7.9 convolution_add_fusion.12
  944.5 8.7 select_add_fusion.8
  953.2 8.5 all-reduce.16.cloned.1.call-done
  974.2 5.5 convolution_convert_fusion.6
  979.7 7.1 convert_element_type.389
  989.7 5.8 convert_element_type.381
  996.8 81.0 %all-reduce.1 = (bf16[2,576]{1,0:T(2,128)(2,1)S(1)}, bf16[1152]{0:T(1024)(128)(2,1)S(1)}, bf16[2304]{0:T(1024)(128)(2,1)S(1)}, bf16[1152]{0:T(1024)(128)(2,1)S(1)}, bf16[3456]{0:T(1024)(128)(2,1)S(1)}) all-reduce(bf16[2,576]{1,0:T(2,128)(2,1)S(1)} %convert_element_type.383, ...), channel_id=1, replica_groups=mesh['dp'=16,'mp'=2] {'dp'}, use_global_device_ids=true, to_apply=%region_30.0 | all-reduce | flops 9216 | bytes 36864 | tf_op jit(solution)/shard_map/psum | solution.py:333
  1080.8 5.7 convolution_convert_fusion.7
  1090.5 541.9 %all-reduce.10.cloned.1.call-done = (bf16[1152,3,576]{0,2,1:T(8,128)(2,1)}, bf16[576,1152]{1,0:T(8,128)(2,1)}, bf16[1152,2304]{1,0:T(8,128)(2,1)}, bf16[2304,1152]{1,0:T(8,128)(2,1)}, bf16[1152,3456]{1,0:T(8,128)(2,1)}) async-done(((bf16[1152,3,576]{0,2,1:T(8,128)(2,1)}, bf16[576,1152]{1,0:T(8,128)(2,1)}, bf16[1152,2304]{1,0:T(8,128)(2,1)}, bf16[2304,1152]{1,0:T(8,128)(2,1)}, bf16[1152,3456]{1,0:T(8,128)(2,1)}), ...) | async-done | bytes 23887888 | tf_op jit(solution)/shard_map/psum | solution.py:332
  1632.4 10.3 convert_element_type.398
  1642.7 5.2 convert_element_type.390
  1648.0 4.8 convert_element_type.394
  (1106 shorter events, 471.0 us)
Async XLA Ops:
  8.1 11.7 slice-start.3
  23.1 951.0 %copy-start.32 = (bf16[8,1152]{1,0:T(8,128)(2,1)S(1)}, bf16[8,1152]{1,0:T(8,128)(2,1)}, u32[]{:S(2)}) copy-start(bf16[8,1152]{1,0:T(8,128)(2,1)} %param.17) | copy-start | bytes 55300
  23.4 33.4 %all-reduce.12.cloned.1.call-start = ((), (), s32[]{:S(2)}) async-start(), calls=%async_computation.1 | async-start | bytes 1179648 | tf_op jit(solution)/shard_map/while/body/eval_jaxpr/psum | solution.py:113
  35.1 58.4 %all-reduce.14.cloned.1.call-start = ((), (), s32[]{:S(2)}) async-start(), calls=%async_computation.2 | async-start | bytes 1179648 | tf_op jit(solution)/shard_map/while/body/eval_jaxpr/psum | solution.py:168
  58.8 12.0 slice-start.5
  73.4 57.6 %all-reduce.16.cloned.1.call-start = ((), (), s32[]{:S(2)}) async-start(), calls=%async_computation.3 | async-start | bytes 2359296 | tf_op jit(solution)/shard_map/while/body/eval_jaxpr/psum | solution.py:127
  73.5 12.7 slice-start.7
  142.5 32.0 %all-reduce.12.cloned.1.call-start = ((), (), s32[]{:S(2)}) async-start(), calls=%async_computation.1 | async-start | bytes 1179648 | tf_op jit(solution)/shard_map/while/body/eval_jaxpr/psum | solution.py:113
  154.3 57.9 %all-reduce.14.cloned.1.call-start = ((), (), s32[]{:S(2)}) async-start(), calls=%async_computation.2 | async-start | bytes 1179648 | tf_op jit(solution)/shard_map/while/body/eval_jaxpr/psum | solution.py:168
  176.5 12.0 slice-start.5
  191.1 58.5 %all-reduce.16.cloned.1.call-start = ((), (), s32[]{:S(2)}) async-start(), calls=%async_computation.3 | async-start | bytes 2359296 | tf_op jit(solution)/shard_map/while/body/eval_jaxpr/psum | solution.py:127
  191.2 10.4 copy-start.2
  191.2 10.4 copy-start.17
  191.2 18.4 %slice-start.7 = ((s8[5308416]{0:T(1024)(128)(4,1)}), s8[4194304]{0:T(1024)(128)(4,1)S(1)}, s32[]{:S(2)}) async-start(s8[5308416]{0:T(1024)(128)(4,1)} %bitcast.263), calls=%async_computation.11 | async-start | bytes 8388608 | tf_op jit(solution)/shard_map/while
  201.6 7.9 slice-start.8
  261.2 32.0 %all-reduce.12.cloned.1.call-start = ((), (), s32[]{:S(2)}) async-start(), calls=%async_computation.1 | async-start | bytes 1179648 | tf_op jit(solution)/shard_map/while/body/eval_jaxpr/psum | solution.py:113
  273.0 57.9 %all-reduce.14.cloned.1.call-start = ((), (), s32[]{:S(2)}) async-start(), calls=%async_computation.2 | async-start | bytes 1179648 | tf_op jit(solution)/shard_map/while/body/eval_jaxpr/psum | solution.py:168
  295.2 12.0 slice-start.5
  309.8 58.5 %all-reduce.16.cloned.1.call-start = ((), (), s32[]{:S(2)}) async-start(), calls=%async_computation.3 | async-start | bytes 2359296 | tf_op jit(solution)/shard_map/while/body/eval_jaxpr/psum | solution.py:127
  309.9 10.4 copy-start.2
  309.9 10.4 copy-start.17
  309.9 18.4 %slice-start.7 = ((s8[5308416]{0:T(1024)(128)(4,1)}), s8[4194304]{0:T(1024)(128)(4,1)S(1)}, s32[]{:S(2)}) async-start(s8[5308416]{0:T(1024)(128)(4,1)} %bitcast.263), calls=%async_computation.11 | async-start | bytes 8388608 | tf_op jit(solution)/shard_map/while
  320.3 7.9 slice-start.8
  379.9 32.0 %all-reduce.12.cloned.1.call-start = ((), (), s32[]{:S(2)}) async-start(), calls=%async_computation.1 | async-start | bytes 1179648 | tf_op jit(solution)/shard_map/while/body/eval_jaxpr/psum | solution.py:113
  391.7 57.9 %all-reduce.14.cloned.1.call-start = ((), (), s32[]{:S(2)}) async-start(), calls=%async_computation.2 | async-start | bytes 1179648 | tf_op jit(solution)/shard_map/while/body/eval_jaxpr/psum | solution.py:168
  413.9 12.0 slice-start.5
  428.5 58.5 %all-reduce.16.cloned.1.call-start = ((), (), s32[]{:S(2)}) async-start(), calls=%async_computation.3 | async-start | bytes 2359296 | tf_op jit(solution)/shard_map/while/body/eval_jaxpr/psum | solution.py:127
  428.5 10.4 copy-start.2
  428.6 10.4 copy-start.17
  428.6 18.4 %slice-start.7 = ((s8[5308416]{0:T(1024)(128)(4,1)}), s8[4194304]{0:T(1024)(128)(4,1)S(1)}, s32[]{:S(2)}) async-start(s8[5308416]{0:T(1024)(128)(4,1)} %bitcast.263), calls=%async_computation.11 | async-start | bytes 8388608 | tf_op jit(solution)/shard_map/while
  498.6 32.0 %all-reduce.12.cloned.1.call-start = ((), (), s32[]{:S(2)}) async-start(), calls=%async_computation.1 | async-start | bytes 1179648 | tf_op jit(solution)/shard_map/while/body/eval_jaxpr/psum | solution.py:113
  510.4 57.9 %all-reduce.14.cloned.1.call-start = ((), (), s32[]{:S(2)}) async-start(), calls=%async_computation.2 | async-start | bytes 1179648 | tf_op jit(solution)/shard_map/while/body/eval_jaxpr/psum | solution.py:168
  532.6 12.0 slice-start.5
  547.2 58.5 %all-reduce.16.cloned.1.call-start = ((), (), s32[]{:S(2)}) async-start(), calls=%async_computation.3 | async-start | bytes 2359296 | tf_op jit(solution)/shard_map/while/body/eval_jaxpr/psum | solution.py:127
  547.2 10.4 copy-start.2
  547.2 10.4 copy-start.17
  547.2 18.4 %slice-start.7 = ((s8[5308416]{0:T(1024)(128)(4,1)}), s8[4194304]{0:T(1024)(128)(4,1)S(1)}, s32[]{:S(2)}) async-start(s8[5308416]{0:T(1024)(128)(4,1)} %bitcast.263), calls=%async_computation.11 | async-start | bytes 8388608 | tf_op jit(solution)/shard_map/while
  557.7 7.9 slice-start.8
  617.3 32.0 %all-reduce.12.cloned.1.call-start = ((), (), s32[]{:S(2)}) async-start(), calls=%async_computation.1 | async-start | bytes 1179648 | tf_op jit(solution)/shard_map/while/body/eval_jaxpr/psum | solution.py:113
  629.0 57.9 %all-reduce.14.cloned.1.call-start = ((), (), s32[]{:S(2)}) async-start(), calls=%async_computation.2 | async-start | bytes 1179648 | tf_op jit(solution)/shard_map/while/body/eval_jaxpr/psum | solution.py:168
  651.2 12.0 slice-start.5
  665.9 58.5 %all-reduce.16.cloned.1.call-start = ((), (), s32[]{:S(2)}) async-start(), calls=%async_computation.3 | async-start | bytes 2359296 | tf_op jit(solution)/shard_map/while/body/eval_jaxpr/psum | solution.py:127
  665.9 10.4 copy-start.2
  665.9 10.4 copy-start.17
  665.9 18.4 %slice-start.7 = ((s8[5308416]{0:T(1024)(128)(4,1)}), s8[4194304]{0:T(1024)(128)(4,1)S(1)}, s32[]{:S(2)}) async-start(s8[5308416]{0:T(1024)(128)(4,1)} %bitcast.263), calls=%async_computation.11 | async-start | bytes 8388608 | tf_op jit(solution)/shard_map/while
  735.9 32.0 %all-reduce.12.cloned.1.call-start = ((), (), s32[]{:S(2)}) async-start(), calls=%async_computation.1 | async-start | bytes 1179648 | tf_op jit(solution)/shard_map/while/body/eval_jaxpr/psum | solution.py:113
  747.7 57.9 %all-reduce.14.cloned.1.call-start = ((), (), s32[]{:S(2)}) async-start(), calls=%async_computation.2 | async-start | bytes 1179648 | tf_op jit(solution)/shard_map/while/body/eval_jaxpr/psum | solution.py:168
  769.9 12.0 slice-start.5
  784.5 58.5 %all-reduce.16.cloned.1.call-start = ((), (), s32[]{:S(2)}) async-start(), calls=%async_computation.3 | async-start | bytes 2359296 | tf_op jit(solution)/shard_map/while/body/eval_jaxpr/psum | solution.py:127
  784.6 10.4 copy-start.2
  784.6 10.4 copy-start.17
  784.6 18.4 %slice-start.7 = ((s8[5308416]{0:T(1024)(128)(4,1)}), s8[4194304]{0:T(1024)(128)(4,1)S(1)}, s32[]{:S(2)}) async-start(s8[5308416]{0:T(1024)(128)(4,1)} %bitcast.263), calls=%async_computation.11 | async-start | bytes 8388608 | tf_op jit(solution)/shard_map/while
  795.0 7.9 slice-start.8
  854.6 32.0 %all-reduce.12.cloned.1.call-start = ((), (), s32[]{:S(2)}) async-start(), calls=%async_computation.1 | async-start | bytes 1179648 | tf_op jit(solution)/shard_map/while/body/eval_jaxpr/psum | solution.py:113
  866.4 57.9 %all-reduce.14.cloned.1.call-start = ((), (), s32[]{:S(2)}) async-start(), calls=%async_computation.2 | async-start | bytes 1179648 | tf_op jit(solution)/shard_map/while/body/eval_jaxpr/psum | solution.py:168
  888.6 12.0 slice-start.5
  903.2 58.5 %all-reduce.16.cloned.1.call-start = ((), (), s32[]{:S(2)}) async-start(), calls=%async_computation.3 | async-start | bytes 2359296 | tf_op jit(solution)/shard_map/while/body/eval_jaxpr/psum | solution.py:127
  903.3 10.4 copy-start.2
  903.3 10.4 copy-start.17
  903.3 18.4 %slice-start.7 = ((s8[5308416]{0:T(1024)(128)(4,1)}), s8[4194304]{0:T(1024)(128)(4,1)S(1)}, s32[]{:S(2)}) async-start(s8[5308416]{0:T(1024)(128)(4,1)} %bitcast.263), calls=%async_computation.11 | async-start | bytes 8388608 | tf_op jit(solution)/shard_map/while
  973.3 659.1 %all-reduce.10.cloned.1.call-start = ((), (), s32[]{:S(2)}) async-start(), calls=%async_computation | async-start | bytes 47775744 | tf_op jit(solution)/shard_map/psum | solution.py:332
  974.2 12.6 slice-start
  974.2 12.6 slice-start.1
  1632.4 10.3 copy-start.25
  (227 other events, 768.4 us)
Sparse Core Ops, SparseCore 0:
  35.3 21.4 all-reduce.11
  73.5 20.0 all-reduce.13
  109.9 21.0 all-reduce.15
  154.4 20.0 all-reduce.11
  191.3 20.0 all-reduce.13
  228.6 21.0 all-reduce.15
  273.1 20.0 all-reduce.11
  309.9 20.0 all-reduce.13
  347.2 21.0 all-reduce.15
  391.8 20.0 all-reduce.11
  428.6 20.0 all-reduce.13
  465.9 21.0 all-reduce.15
  510.5 20.0 all-reduce.11
  547.3 20.0 all-reduce.13
  584.6 21.0 all-reduce.15
  629.2 20.0 all-reduce.11
  666.0 20.0 all-reduce.13
  703.3 21.0 all-reduce.15
  747.8 20.0 all-reduce.11
  784.7 20.0 all-reduce.13
  822.0 21.0 all-reduce.15
  866.5 20.0 all-reduce.11
  903.3 20.0 all-reduce.13
  940.7 21.0 all-reduce.15
Sparse Core Ops, SparseCore 1:
  996.8 635.5 all-reduce.9
where the time goes:
time: 1670 us
  waiting for transfers between devices  759 us (45%)
  matrix products  505 us (30%)
  other arithmetic  245 us (15%)
  blocking collectives  86.5 us (5%)
  local copies, waits for them, and re-layouts  44.8 us (3%)
    psum x1, waiting for transfers between devices, on_device(): lax.psum(grad_w_qkv.astype(jnp.bfloat16), 'dp').astype(jnp.float32)  542 us
    dot_general x33, matrix products, inner_rows(): lax.dot_general(left, right, (((0,), (0,)), ((), ())), preferred_element_...  243 us
    psum x8, waiting for transfers between devices, forward(): lax.psum(partial_value.astype(jnp.bfloat16), 'mp').astype(jnp.float32)  139 us
    dot_general x33, matrix products, outer_cols(): lax.dot_general(left, right, (((1,), (1,)), ((), ())), preferred_element_...  120 us
    psum x1, blocking collectives, on_device(): lax.psum(grad_b_qv.astype(jnp.bfloat16), 'dp').astype(jnp.float32)  81 us
    psum x8, waiting for transfers between devices, forward(): lax.psum(partial_mlp.astype(jnp.bfloat16), 'mp').astype(jnp.float32)  72.8 us
    dot_general x8, matrix products, forward(): jnp.dot(normed_mlp, w_up, preferred_element_type=jnp.float32)  35.7 us
  transfers between devices with their start and end apart: 25, of which 18 were waited for; matrix products, arithmetic and copies ran while one was open for 17% of the time, Pallas kernels for 0%

commit v1 on v0

--- a/solution.py
+++ b/solution.py
@@ -124,7 +124,9 @@
     if repeat:
         summed_mlp = lax.psum(partial_mlp.astype(jnp.bfloat16), "mp").astype(jnp.float32)
     else:
-        summed_mlp = lax.psum(partial_mlp.astype(jnp.bfloat16), "mp").astype(jnp.float32)
+        summed_mlp = jnp.sum(lax.all_gather(partial_mlp.astype(jnp.bfloat16), "mp"), axis=0).astype(
+            jnp.float32
+        )
     mlp_out = (summed_mlp + b_down.astype(jnp.float32)).reshape(slot_count, seq_len, model_dim)
     output = residual + gate_mlp * mlp_out
     return {

time: 1670 us -> 1730 us (1.036)
  waiting for transfers between devices: 759 us -> 804 us
  matrix products: 505 us -> 484 us
    psum x8, waiting for transfers between devices: 72.8 us -> 112 us  [image_pass(): lax.psum(part_normed.astype(jnp.bfloat16), 'mp').astype(jnp.float32)]
    dot_general x33, matrix products: 120 us -> 99.9 us  [outer_cols(): lax.dot_general(left, right, (((1,), (1,)), ((), ())), preferred_element_...]
    while x536 -> x520, local copies, waits for them, and re-layouts: 29.1 us -> 34.6 us
  transfers between devices with their start and end apart: 25 -> 33, of which waited for: 18 -> 18; matrix products, arithmetic and copies ran while one was open for 17% -> 23% of each run, Pallas kernels for 0% -> 0%
where the time goes in v1:
time: 1730 us; the launch traced here: 1720 us
  waiting for transfers between devices  804 us (46%)
  matrix products  484 us (28%)
  other arithmetic  252 us (15%)
  blocking collectives  86.6 us (5%)
  local copies, waits for them, and re-layouts  50.3 us (3%)
  loops' own time  26 us (2%)
    psum x1, waiting for transfers between devices, on_device(): lax.psum(grad_w_qkv.astype(jnp.bfloat16), 'dp').astype(jnp.float32)  542 us
    dot_general x33, matrix products, inner_rows(): lax.dot_general(left, right, (((0,), (0,)), ((), ())), preferred_element_...  242 us
    psum x8, waiting for transfers between devices, forward(): lax.psum(partial_value.astype(jnp.bfloat16), 'mp').astype(jnp.float32)  139 us
    psum x8, waiting for transfers between devices, image_pass(): lax.psum(part_normed.astype(jnp.bfloat16), 'mp').astype(jnp.float32)  112 us
    dot_general x33, matrix products, outer_cols(): lax.dot_general(left, right, (((1,), (1,)), ((), ())), preferred_element_...  99.9 us
    psum x1, blocking collectives, on_device(): lax.psum(grad_b_qv.astype(jnp.bfloat16), 'dp').astype(jnp.float32)  81 us
    dot_general x8, matrix products, forward(): jnp.dot(normed_mlp, w_up, preferred_element_type=jnp.float32)  35.7 us
    while x520, local copies, waits for them, and re-layouts  34.6 us
  transfers between devices with their start and end apart: 33, of which 18 were waited for; matrix products, arithmetic and copies ran while one was open for 23% of the time, Pallas kernels for 0%

profile of v1, /device:TPU:0, one launch (start us, length us, event | category | flops | bytes accessed | tf_op | source)
XLA Modules:
  0.0 1719.5 jit_solution(8657441784525560823)
XLA Ops:
  8.1 7.3 convert_element_type.497
  23.3 1003.8 %while.36 = (s32[]{:T(128)}, bf16[8,256,1152]{2,1,0:T(8,128)(2,1)}, f32[8,256,1152]{2,1,0:T(8,128)}, bf16[8,6912]{1,0:T(8,128)(2,1)}, f32[1152,3,576]{0,2,1:T(8,...) while((s32[]{:T(128)}, bf16[8,256,1152]{2,1,0:T(8,128)(2,1)}, ...), condition=%wide.region_28.0_spmd.clone, body=%wide.region_0.28_spmd.clone.sunk | while | flops 12777687040 | bytes 321953728 | solution.py:275
  55.4 18.6 %all-reduce.12.cloned.1.call-done = bf16[256,1152]{1,0:T(8,128)(2,1)} async-done(((bf16[256,1152]{1,0:T(8,128)(2,1)}), bf16[256,1152]{1,0:T(8,128)(2,1)}) %all-reduce.12.cloned.1.call-update) | async-done | bytes 589840 | tf_op jit(solution)/shard_map/while/body/eval_jaxpr/psum | solution.py:113
  76.1 4.5 convolution_add_fusion.9
  80.6 6.4 convert_reduce_fusion.14
  90.8 7.3 convolution_add_fusion.11
  98.1 5.4 convolution_add_fusion.12
  106.1 4.7 all-reduce.14.cloned.1.call-done
  129.1 6.1 select_add_fusion.8
  136.6 16.1 all-reduce.16.cloned.1.call-done
  178.6 17.2 %all-reduce.12.cloned.1.call-done = bf16[256,1152]{1,0:T(8,128)(2,1)} async-done(((bf16[256,1152]{1,0:T(8,128)(2,1)}), bf16[256,1152]{1,0:T(8,128)(2,1)}) %all-reduce.12.cloned.1.call-update) | async-done | bytes 589840 | tf_op jit(solution)/shard_map/while/body/eval_jaxpr/psum | solution.py:113
  202.4 6.4 convert_reduce_fusion.14
  212.5 10.4 convolution_add_fusion.11
  222.9 7.9 convolution_add_fusion.12
  252.7 8.5 select_add_fusion.8
  262.5 13.8 all-reduce.16.cloned.1.call-done
  302.2 17.2 %all-reduce.12.cloned.1.call-done = bf16[256,1152]{1,0:T(8,128)(2,1)} async-done(((bf16[256,1152]{1,0:T(8,128)(2,1)}), bf16[256,1152]{1,0:T(8,128)(2,1)}) %all-reduce.12.cloned.1.call-update) | async-done | bytes 589840 | tf_op jit(solution)/shard_map/while/body/eval_jaxpr/psum | solution.py:113
  321.5 4.5 convolution_add_fusion.9
  326.0 6.4 convert_reduce_fusion.14
  336.1 10.4 convolution_add_fusion.11
  346.6 7.9 convolution_add_fusion.12
  376.1 8.5 select_add_fusion.8
  385.9 13.7 all-reduce.16.cloned.1.call-done
  425.5 17.2 %all-reduce.12.cloned.1.call-done = bf16[256,1152]{1,0:T(8,128)(2,1)} async-done(((bf16[256,1152]{1,0:T(8,128)(2,1)}), bf16[256,1152]{1,0:T(8,128)(2,1)}) %all-reduce.12.cloned.1.call-update) | async-done | bytes 589840 | tf_op jit(solution)/shard_map/while/body/eval_jaxpr/psum | solution.py:113
  449.3 6.4 convert_reduce_fusion.14
  459.4 10.4 convolution_add_fusion.11
  469.8 7.9 convolution_add_fusion.12
  499.4 8.5 select_add_fusion.8
  509.2 13.7 all-reduce.16.cloned.1.call-done
  548.8 17.2 %all-reduce.12.cloned.1.call-done = bf16[256,1152]{1,0:T(8,128)(2,1)} async-done(((bf16[256,1152]{1,0:T(8,128)(2,1)}), bf16[256,1152]{1,0:T(8,128)(2,1)}) %all-reduce.12.cloned.1.call-update) | async-done | bytes 589840 | tf_op jit(solution)/shard_map/while/body/eval_jaxpr/psum | solution.py:113
  572.5 6.4 convert_reduce_fusion.14
  582.7 10.4 convolution_add_fusion.11
  593.1 7.9 convolution_add_fusion.12
  622.7 8.5 select_add_fusion.8
  632.5 13.7 all-reduce.16.cloned.1.call-done
  672.1 17.2 %all-reduce.12.cloned.1.call-done = bf16[256,1152]{1,0:T(8,128)(2,1)} async-done(((bf16[256,1152]{1,0:T(8,128)(2,1)}), bf16[256,1152]{1,0:T(8,128)(2,1)}) %all-reduce.12.cloned.1.call-update) | async-done | bytes 589840 | tf_op jit(solution)/shard_map/while/body/eval_jaxpr/psum | solution.py:113
  691.3 4.5 convolution_add_fusion.9
  695.8 6.4 convert_reduce_fusion.14
  706.0 10.4 convolution_add_fusion.11
  716.4 7.9 convolution_add_fusion.12
  746.0 8.5 select_add_fusion.8
  755.8 13.7 all-reduce.16.cloned.1.call-done
  795.4 17.2 %all-reduce.12.cloned.1.call-done = bf16[256,1152]{1,0:T(8,128)(2,1)} async-done(((bf16[256,1152]{1,0:T(8,128)(2,1)}), bf16[256,1152]{1,0:T(8,128)(2,1)}) %all-reduce.12.cloned.1.call-update) | async-done | bytes 589840 | tf_op jit(solution)/shard_map/while/body/eval_jaxpr/psum | solution.py:113
  819.1 6.4 convert_reduce_fusion.14
  829.3 10.4 convolution_add_fusion.11
  839.7 7.9 convolution_add_fusion.12
  869.4 8.5 select_add_fusion.8
  879.2 13.8 all-reduce.16.cloned.1.call-done
  919.0 17.2 %all-reduce.12.cloned.1.call-done = bf16[256,1152]{1,0:T(8,128)(2,1)} async-done(((bf16[256,1152]{1,0:T(8,128)(2,1)}), bf16[256,1152]{1,0:T(8,128)(2,1)}) %all-reduce.12.cloned.1.call-update) | async-done | bytes 589840 | tf_op jit(solution)/shard_map/while/body/eval_jaxpr/psum | solution.py:113
  938.2 4.5 convolution_add_fusion.9
  942.7 6.4 convert_reduce_fusion.14
  952.9 10.4 convolution_add_fusion.11
  963.3 7.9 convolution_add_fusion.12
  993.0 8.5 select_add_fusion.8
  1002.8 13.8 all-reduce.16.cloned.1.call-done
  1028.0 5.5 convolution_convert_fusion.6
  1033.5 7.1 convert_element_type.513
  1043.5 5.8 convert_element_type.505
  1050.5 81.0 %all-reduce.1 = (bf16[2,576]{1,0:T(2,128)(2,1)S(1)}, bf16[1152]{0:T(1024)(128)(2,1)S(1)}, bf16[2304]{0:T(1024)(128)(2,1)S(1)}, bf16[1152]{0:T(1024)(128)(2,1)S(1)}, bf16[3456]{0:T(1024)(128)(2,1)S(1)}) all-reduce(bf16[2,576]{1,0:T(2,128)(2,1)S(1)} %convert_element_type.507, ...), channel_id=1, replica_groups=mesh['dp'=16,'mp'=2] {'dp'}, use_global_device_ids=true, to_apply=%region_31.0 | all-reduce | flops 9216 | bytes 36864 | tf_op jit(solution)/shard_map/psum | solution.py:335
  1134.6 5.7 convolution_convert_fusion.7
  1144.3 541.9 %all-reduce.10.cloned.1.call-done = (bf16[1152,3,576]{0,2,1:T(8,128)(2,1)}, bf16[576,1152]{1,0:T(8,128)(2,1)}, bf16[1152,2304]{1,0:T(8,128)(2,1)}, bf16[2304,1152]{1,0:T(8,128)(2,1)}, bf16[1152,3456]{1,0:T(8,128)(2,1)}) async-done(((bf16[1152,3,576]{0,2,1:T(8,128)(2,1)}, bf16[576,1152]{1,0:T(8,128)(2,1)}, bf16[1152,2304]{1,0:T(8,128)(2,1)}, bf16[2304,1152]{1,0:T(8,128)(2,1)}, bf16[1152,3456]{1,0:T(8,128)(2,1)}), ...) | async-done | bytes 23887888 | tf_op jit(solution)/shard_map/psum | solution.py:334
  1686.2 10.3 convert_element_type.522
  1696.5 5.2 convert_element_type.514
  1701.7 4.8 convert_element_type.518
  (1122 shorter events, 470.7 us)
Async XLA Ops:
  8.1 11.7 slice-start.3
  23.3 1004.7 %copy-start.30 = (bf16[8,1152]{1,0:T(8,128)(2,1)S(1)}, bf16[8,1152]{1,0:T(8,128)(2,1)}, u32[]{:S(2)}) copy-start(bf16[8,1152]{1,0:T(8,128)(2,1)} %param.17) | copy-start | bytes 55300
  39.8 34.2 %all-reduce.12.cloned.1.call-start = ((), (), s32[]{:S(2)}) async-start(), calls=%async_computation.1 | async-start | bytes 1179648 | tf_op jit(solution)/shard_map/while/body/eval_jaxpr/psum | solution.py:113
  52.4 58.4 %all-reduce.14.cloned.1.call-start = ((), (), s32[]{:S(2)}) async-start(), calls=%async_computation.3 | async-start | bytes 1179648 | tf_op jit(solution)/shard_map/while/body/eval_jaxpr/psum | solution.py:170
  76.1 12.0 slice-start.5
  90.7 37.9 %all-gather.6.cloned.1.call-start = ((), (), s32[]{:S(2)}) async-start(), calls=%async_computation.2 | async-start | bytes 1769472 | tf_op jit(solution)/shard_map/while/body/eval_jaxpr/all_gather | solution.py:127
  90.8 12.7 slice-start.7
  128.6 24.2 %all-reduce.16.cloned.1.call-start = ((), (), s32[]{:S(2)}) async-start(), calls=%async_computation.4 | async-start | bytes 2359296 | tf_op jit(solution)/shard_map/while/body/eval_jaxpr/psum | solution.py:208
  163.1 32.7 %all-reduce.12.cloned.1.call-start = ((), (), s32[]{:S(2)}) async-start(), calls=%async_computation.1 | async-start | bytes 1179648 | tf_op jit(solution)/shard_map/while/body/eval_jaxpr/psum | solution.py:113
  175.6 58.0 %all-reduce.14.cloned.1.call-start = ((), (), s32[]{:S(2)}) async-start(), calls=%async_computation.3 | async-start | bytes 1179648 | tf_op jit(solution)/shard_map/while/body/eval_jaxpr/psum | solution.py:170
  197.8 12.0 slice-start.5
  212.5 39.4 %all-gather.6.cloned.1.call-start = ((), (), s32[]{:S(2)}) async-start(), calls=%async_computation.2 | async-start | bytes 1769472 | tf_op jit(solution)/shard_map/while/body/eval_jaxpr/all_gather | solution.py:127
  212.5 10.4 copy-start.3
  212.5 10.4 copy-start.16
  212.5 18.3 %slice-start.7 = ((s8[5308416]{0:T(1024)(128)(4,1)}), s8[4194304]{0:T(1024)(128)(4,1)S(1)}, s32[]{:S(2)}) async-start(s8[5308416]{0:T(1024)(128)(4,1)} %bitcast.262), calls=%async_computation.12 | async-start | bytes 8388608 | tf_op jit(solution)/shard_map/while
  251.9 24.4 %all-reduce.16.cloned.1.call-start = ((), (), s32[]{:S(2)}) async-start(), calls=%async_computation.4 | async-start | bytes 2359296 | tf_op jit(solution)/shard_map/while/body/eval_jaxpr/psum | solution.py:208
  286.7 32.7 %all-reduce.12.cloned.1.call-start = ((), (), s32[]{:S(2)}) async-start(), calls=%async_computation.1 | async-start | bytes 1179648 | tf_op jit(solution)/shard_map/while/body/eval_jaxpr/psum | solution.py:113
  299.2 58.0 %all-reduce.14.cloned.1.call-start = ((), (), s32[]{:S(2)}) async-start(), calls=%async_computation.3 | async-start | bytes 1179648 | tf_op jit(solution)/shard_map/while/body/eval_jaxpr/psum | solution.py:170
  321.5 12.0 slice-start.5
  336.1 39.5 %all-gather.6.cloned.1.call-start = ((), (), s32[]{:S(2)}) async-start(), calls=%async_computation.2 | async-start | bytes 1769472 | tf_op jit(solution)/shard_map/while/body/eval_jaxpr/all_gather | solution.py:127
  336.1 10.4 copy-start.3
  336.1 10.4 copy-start.16
  336.1 18.4 %slice-start.7 = ((s8[5308416]{0:T(1024)(128)(4,1)}), s8[4194304]{0:T(1024)(128)(4,1)S(1)}, s32[]{:S(2)}) async-start(s8[5308416]{0:T(1024)(128)(4,1)} %bitcast.262), calls=%async_computation.12 | async-start | bytes 8388608 | tf_op jit(solution)/shard_map/while
  375.5 24.1 %all-reduce.16.cloned.1.call-start = ((), (), s32[]{:S(2)}) async-start(), calls=%async_computation.4 | async-start | bytes 2359296 | tf_op jit(solution)/shard_map/while/body/eval_jaxpr/psum | solution.py:208
  410.0 32.7 %all-reduce.12.cloned.1.call-start = ((), (), s32[]{:S(2)}) async-start(), calls=%async_computation.1 | async-start | bytes 1179648 | tf_op jit(solution)/shard_map/while/body/eval_jaxpr/psum | solution.py:113
  422.5 58.0 %all-reduce.14.cloned.1.call-start = ((), (), s32[]{:S(2)}) async-start(), calls=%async_computation.3 | async-start | bytes 1179648 | tf_op jit(solution)/shard_map/while/body/eval_jaxpr/psum | solution.py:170
  444.7 12.0 slice-start.5
  459.4 39.4 %all-gather.6.cloned.1.call-start = ((), (), s32[]{:S(2)}) async-start(), calls=%async_computation.2 | async-start | bytes 1769472 | tf_op jit(solution)/shard_map/while/body/eval_jaxpr/all_gather | solution.py:127
  459.4 10.4 copy-start.3
  459.4 18.3 %slice-start.7 = ((s8[5308416]{0:T(1024)(128)(4,1)}), s8[4194304]{0:T(1024)(128)(4,1)S(1)}, s32[]{:S(2)}) async-start(s8[5308416]{0:T(1024)(128)(4,1)} %bitcast.262), calls=%async_computation.12 | async-start | bytes 8388608 | tf_op jit(solution)/shard_map/while
  498.8 24.1 %all-reduce.16.cloned.1.call-start = ((), (), s32[]{:S(2)}) async-start(), calls=%async_computation.4 | async-start | bytes 2359296 | tf_op jit(solution)/shard_map/while/body/eval_jaxpr/psum | solution.py:208
  533.3 32.7 %all-reduce.12.cloned.1.call-start = ((), (), s32[]{:S(2)}) async-start(), calls=%async_computation.1 | async-start | bytes 1179648 | tf_op jit(solution)/shard_map/while/body/eval_jaxpr/psum | solution.py:113
  545.8 58.0 %all-reduce.14.cloned.1.call-start = ((), (), s32[]{:S(2)}) async-start(), calls=%async_computation.3 | async-start | bytes 1179648 | tf_op jit(solution)/shard_map/while/body/eval_jaxpr/psum | solution.py:170
  568.0 12.0 slice-start.5
  582.6 39.4 %all-gather.6.cloned.1.call-start = ((), (), s32[]{:S(2)}) async-start(), calls=%async_computation.2 | async-start | bytes 1769472 | tf_op jit(solution)/shard_map/while/body/eval_jaxpr/all_gather | solution.py:127
  582.7 10.4 copy-start.3
  582.7 18.3 %slice-start.7 = ((s8[5308416]{0:T(1024)(128)(4,1)}), s8[4194304]{0:T(1024)(128)(4,1)S(1)}, s32[]{:S(2)}) async-start(s8[5308416]{0:T(1024)(128)(4,1)} %bitcast.262), calls=%async_computation.12 | async-start | bytes 8388608 | tf_op jit(solution)/shard_map/while
  622.1 24.1 %all-reduce.16.cloned.1.call-start = ((), (), s32[]{:S(2)}) async-start(), calls=%async_computation.4 | async-start | bytes 2359296 | tf_op jit(solution)/shard_map/while/body/eval_jaxpr/psum | solution.py:208
  656.6 32.7 %all-reduce.12.cloned.1.call-start = ((), (), s32[]{:S(2)}) async-start(), calls=%async_computation.1 | async-start | bytes 1179648 | tf_op jit(solution)/shard_map/while/body/eval_jaxpr/psum | solution.py:113
  669.1 58.0 %all-reduce.14.cloned.1.call-start = ((), (), s32[]{:S(2)}) async-start(), calls=%async_computation.3 | async-start | bytes 1179648 | tf_op jit(solution)/shard_map/while/body/eval_jaxpr/psum | solution.py:170
  691.3 12.0 slice-start.5
  705.9 39.5 %all-gather.6.cloned.1.call-start = ((), (), s32[]{:S(2)}) async-start(), calls=%async_computation.2 | async-start | bytes 1769472 | tf_op jit(solution)/shard_map/while/body/eval_jaxpr/all_gather | solution.py:127
  706.0 10.4 copy-start.3
  706.0 10.4 copy-start.16
  706.0 18.4 %slice-start.7 = ((s8[5308416]{0:T(1024)(128)(4,1)}), s8[4194304]{0:T(1024)(128)(4,1)S(1)}, s32[]{:S(2)}) async-start(s8[5308416]{0:T(1024)(128)(4,1)} %bitcast.262), calls=%async_computation.12 | async-start | bytes 8388608 | tf_op jit(solution)/shard_map/while
  745.4 24.1 %all-reduce.16.cloned.1.call-start = ((), (), s32[]{:S(2)}) async-start(), calls=%async_computation.4 | async-start | bytes 2359296 | tf_op jit(solution)/shard_map/while/body/eval_jaxpr/psum | solution.py:208
  779.9 32.7 %all-reduce.12.cloned.1.call-start = ((), (), s32[]{:S(2)}) async-start(), calls=%async_computation.1 | async-start | bytes 1179648 | tf_op jit(solution)/shard_map/while/body/eval_jaxpr/psum | solution.py:113
  792.4 58.0 %all-reduce.14.cloned.1.call-start = ((), (), s32[]{:S(2)}) async-start(), calls=%async_computation.3 | async-start | bytes 1179648 | tf_op jit(solution)/shard_map/while/body/eval_jaxpr/psum | solution.py:170
  814.6 12.0 slice-start.5
  829.2 39.4 %all-gather.6.cloned.1.call-start = ((), (), s32[]{:S(2)}) async-start(), calls=%async_computation.2 | async-start | bytes 1769472 | tf_op jit(solution)/shard_map/while/body/eval_jaxpr/all_gather | solution.py:127
  829.3 10.4 copy-start.3
  829.3 18.3 %slice-start.7 = ((s8[5308416]{0:T(1024)(128)(4,1)}), s8[4194304]{0:T(1024)(128)(4,1)S(1)}, s32[]{:S(2)}) async-start(s8[5308416]{0:T(1024)(128)(4,1)} %bitcast.262), calls=%async_computation.12 | async-start | bytes 8388608 | tf_op jit(solution)/shard_map/while
  868.7 24.4 %all-reduce.16.cloned.1.call-start = ((), (), s32[]{:S(2)}) async-start(), calls=%async_computation.4 | async-start | bytes 2359296 | tf_op jit(solution)/shard_map/while/body/eval_jaxpr/psum | solution.py:208
  903.5 32.7 %all-reduce.12.cloned.1.call-start = ((), (), s32[]{:S(2)}) async-start(), calls=%async_computation.1 | async-start | bytes 1179648 | tf_op jit(solution)/shard_map/while/body/eval_jaxpr/psum | solution.py:113
  916.0 58.0 %all-reduce.14.cloned.1.call-start = ((), (), s32[]{:S(2)}) async-start(), calls=%async_computation.3 | async-start | bytes 1179648 | tf_op jit(solution)/shard_map/while/body/eval_jaxpr/psum | solution.py:170
  938.2 12.0 slice-start.5
  952.8 39.5 %all-gather.6.cloned.1.call-start = ((), (), s32[]{:S(2)}) async-start(), calls=%async_computation.2 | async-start | bytes 1769472 | tf_op jit(solution)/shard_map/while/body/eval_jaxpr/all_gather | solution.py:127
  952.9 10.4 copy-start.3
  952.9 10.4 copy-start.16
  952.9 18.4 %slice-start.7 = ((s8[5308416]{0:T(1024)(128)(4,1)}), s8[4194304]{0:T(1024)(128)(4,1)S(1)}, s32[]{:S(2)}) async-start(s8[5308416]{0:T(1024)(128)(4,1)} %bitcast.262), calls=%async_computation.12 | async-start | bytes 8388608 | tf_op jit(solution)/shard_map/while
  992.3 24.4 %all-reduce.16.cloned.1.call-start = ((), (), s32[]{:S(2)}) async-start(), calls=%async_computation.4 | async-start | bytes 2359296 | tf_op jit(solution)/shard_map/while/body/eval_jaxpr/psum | solution.py:208
  1027.1 659.1 %all-reduce.10.cloned.1.call-start = ((), (), s32[]{:S(2)}) async-start(), calls=%async_computation | async-start | bytes 47775744 | tf_op jit(solution)/shard_map/psum | solution.py:334
  1027.9 12.6 slice-start
  1028.0 12.6 slice-start.1
  (227 other events, 783.3 us)
Sparse Core Ops, SparseCore 0:
  52.5 21.4 all-reduce.11
  90.8 20.0 all-reduce.13
  112.5 10.3 all-gather.5
  131.6 21.1 all-reduce.15
  175.8 20.0 all-reduce.11
  212.6 20.0 all-reduce.13
  234.2 10.4 all-gather.5
  255.2 21.0 all-reduce.15
  299.4 20.0 all-reduce.11
  336.2 20.0 all-reduce.13
  357.9 10.3 all-gather.5
  378.5 21.0 all-reduce.15
  422.7 20.0 all-reduce.11
  459.5 20.0 all-reduce.13
  481.0 10.3 all-gather.5
  501.8 21.0 all-reduce.15
  545.9 20.0 all-reduce.11
  582.8 20.0 all-reduce.13
  604.4 10.4 all-gather.5
  625.1 21.0 all-reduce.15
  669.2 20.0 all-reduce.11
  706.1 20.0 all-reduce.13
  727.7 10.3 all-gather.5
  748.4 21.0 all-reduce.15
  792.5 20.0 all-reduce.11
  829.3 20.0 all-reduce.13
  850.9 10.3 all-gather.5
  872.0 21.0 all-reduce.15
  916.1 20.0 all-reduce.11
  952.9 20.0 all-reduce.13
  974.6 10.3 all-gather.5
  995.6 21.0 all-reduce.15
Sparse Core Ops, SparseCore 1:
  1050.6 635.5 all-reduce.9
